TPU v7x, 32 devices: a whole 2x2x4 slice. The times are simulated.
32 devices in a mesh: groups: 2 (over x), worker: 2 (over core), tensor: 8 (over z, y).
Axes of the slice: x: 2, y: 2, z: 4, core: 2. Of those that a mesh axis runs over, the one named last changes fastest.
Arguments:
- tokens: bfloat16 [1024, 8192], P(('groups', 'worker'), 'tensor'), parts along dimension 0, may hold values from -6 to 6
- norm_gain: float32 [8192], replicated, may hold values from 0.5 to 1.5
- query_weight: bfloat16 [8192, 8192], P(None, 'tensor'), may hold values from -0.0625 to 0.0625
- key_weight: bfloat16 [8192, 1024], P(None, 'tensor'), may hold values from -0.15625 to 0.15625
- value_weight: bfloat16 [8192, 1024], P(None, 'tensor'), may hold values from -0.0625 to 0.0625
- output_weight: bfloat16 [8192, 8192], P('tensor'), may hold values from -0.0625 to 0.0625
- cached_blocks: bfloat16 [8, 1024, 2, 1024], P(('groups', 'worker'), 'tensor'), parts along dimension 0
- cache_length: int32 [8], P('groups'), parts along dimension 0, may hold values from 256 to 1024, as said below
- block_table: int32 [8, 64], P('groups'), parts along dimension 0, may hold values from 0 to 63, each once within a row
- destination: int32 [8], P('groups'), parts along dimension 0, may hold values from 0 to 1, as said below
Outputs:
- attended: bfloat16 [4, 3, 128, 8192], P(('groups', 'worker'), None, None, 'tensor'), parts along dimension 0
There are 2 independent parts, one for each index of `groups`. A program takes and returns all parts, laid end to end along the dimension named above; an argument that names none is the same for every part. Nothing has to cross between parts.
Inputs may be any that keep to these rules, and one draw needn't show every extreme that they name: Exactly 3 sequences have one destination, the others the other; which one is drawn. `cache_length`: some sequence has exactly 1024 cached tokens.
All inputs are finite; a program needn't handle non-finite values.
Results may differ from a plain program's by a relative error of at most 0.02.
The roundings to bfloat16 on the way count: a program that leaves them out, or rounds other values in their place, can miss the bound.
Values may be sent and summed in bfloat16 or wider, within the bound.
No kernel may reach another device: no remote copies, remote signals or barrier semaphores. Data moves between devices by JAX's collectives and lax.ppermute only.
A program may use at most 128 MiB of HBM per device.

v0:
```python
import math
import jax
import jax.numpy as jnp
from jax import lax
from jax.sharding import PartitionSpec as P

D = 8192
KVH = 8
HD = 128
NEW = 128
BLK = 16
CAP = 3
epsilon = 1e-05


def from_partner(block, axis, bit):
    count = lax.axis_size(axis)
    route = []
    for low in range(count):
        high = low | 1 << bit
        if high != low and high < count:
            route += [(low, high), (high, low)]
    return lax.ppermute(block, axis, route)


def rotate(values, positions):
    halfway = HD // 2
    inverse = 500000.0 ** (-(jnp.arange(halfway, dtype=jnp.float32) * 2.0 / HD))
    angles = positions[:, None] * inverse[None, :]
    cosine_table = jnp.concatenate([jnp.cos(angles), jnp.cos(angles)], axis=-1)[:, None, :]
    sine_table = jnp.concatenate([jnp.sin(angles), jnp.sin(angles)], axis=-1)[:, None, :]
    turned = jnp.concatenate([-values[..., halfway:], values[..., :halfway]], axis=-1)
    return values * cosine_table + turned * sine_table


def attend(
    token_rows,
    blocks,
    lengths,
    tables,
    norm_gain,
    query_weight,
    key_weight,
    value_weight,
    output_weight,
):
    tensor_count = lax.axis_size("tensor")
    tensor_index = lax.axis_index("tensor")
    group_width = tensor_count // KVH
    bit_count = group_width.bit_length() - 1
    seq_count = blocks.shape[0]
    total = token_rows.shape[0]
    query_cols = query_weight.shape[1]
    widened = lax.all_gather(token_rows, "tensor", axis=1, tiled=True).astype(jnp.float32)
    scaled = (widened * norm_gain[None, :]).astype(jnp.bfloat16)
    query_sum = jnp.dot(scaled, query_weight, preferred_element_type=jnp.float32)
    key_sum = jnp.dot(scaled, key_weight, preferred_element_type=jnp.float32)
    value_sum = jnp.dot(scaled, value_weight, preferred_element_type=jnp.float32)
    squares = jnp.sum(widened * widened, axis=1)
    factor = lax.rsqrt(squares / D + epsilon)[:, None]
    positions = (
        (lengths[:, None] + jnp.arange(NEW, dtype=jnp.int32)[None, :])
        .reshape(total)
        .astype(jnp.float32)
    )
    heads_here = query_cols // HD
    queries = rotate((query_sum * factor).reshape(total, heads_here, HD), positions).astype(
        jnp.bfloat16
    )
    key_full = (key_sum * factor).astype(jnp.bfloat16)
    value_full = (value_sum * factor).astype(jnp.bfloat16)
    for bit in range(bit_count):
        other_key, other_value = from_partner((key_full, value_full), "tensor", bit)
        upper = tensor_index // (1 << bit) % 2 == 1
        key_full = jnp.where(
            upper,
            jnp.concatenate([other_key, key_full], axis=1),
            jnp.concatenate([key_full, other_key], axis=1),
        )
        value_full = jnp.where(
            upper,
            jnp.concatenate([other_value, value_full], axis=1),
            jnp.concatenate([value_full, other_value], axis=1),
        )
    new_key = rotate(key_full.astype(jnp.float32)[:, None, :], positions)[:, 0, :].astype(
        jnp.bfloat16
    )
    fresh_keys = new_key.reshape(seq_count, NEW, HD)
    fresh_values = value_full.reshape(seq_count, NEW, HD)
    local_tokens = blocks.shape[1]
    inverse_root = 1.0 / math.sqrt(HD)
    query_blocks = queries.reshape(seq_count, NEW, heads_here, HD)
    causal = jnp.arange(NEW)[:, None] >= jnp.arange(NEW)[None, :]
    spread = jnp.repeat(
        blocks.reshape(seq_count, local_tokens, 2, KVH, HD), tensor_count // KVH, axis=3
    )
    arrived = lax.all_to_all(spread, "tensor", split_axis=3, concat_axis=1, tiled=True)
    context = arrived.shape[1]
    old_key = arrived[:, :, 0, 0, :]
    old_value = arrived[:, :, 1, 0, :]
    stored = jnp.arange(context, dtype=jnp.int32)
    logical = jnp.take(tables, stored // BLK, axis=1) * BLK + stored % BLK
    visible = logical < lengths[:, None]
    old_scores = (
        jnp.einsum("sqhd,skd->shqk", query_blocks, old_key, preferred_element_type=jnp.float32)
        * inverse_root
    )
    old_scores = jnp.where(visible[:, None, None, :], old_scores, -1e30)
    new_scores = (
        jnp.einsum("sqhd,skd->shqk", query_blocks, fresh_keys, preferred_element_type=jnp.float32)
        * inverse_root
    )
    new_scores = jnp.where(causal[None, None], new_scores, -1e30)
    largest = jnp.maximum(jnp.max(old_scores, axis=3), jnp.max(new_scores, axis=3))[..., None]
    old_expo = jnp.exp(old_scores - largest)
    new_expo = jnp.exp(new_scores - largest)
    denominator = (jnp.sum(old_expo, axis=3) + jnp.sum(new_expo, axis=3))[..., None]
    old_probs = (old_expo / denominator).astype(jnp.bfloat16)
    new_probs = (new_expo / denominator).astype(jnp.bfloat16)
    mixture = jnp.einsum("shqk,skd->sqhd", old_probs, old_value, preferred_element_type=jnp.float32)
    mixture = mixture + jnp.einsum(
        "shqk,skd->sqhd", new_probs, fresh_values, preferred_element_type=jnp.float32
    )
    attended_rows = mixture.astype(jnp.bfloat16).reshape(total, heads_here * HD)
    partial_value = jnp.dot(attended_rows, output_weight, preferred_element_type=jnp.float32)
    summed = lax.psum_scatter(partial_value, "tensor", scatter_dimension=1, tiled=True)
    return summed.astype(jnp.bfloat16)


def local(
    tokens,
    norm_gain,
    query_weight,
    key_weight,
    value_weight,
    output_weight,
    cached_blocks,
    cache_length,
    block_table,
    destination,
):
    worker_index = lax.axis_index("worker")
    seq_total = destination.shape[0]
    belongs = (destination == worker_index).astype(jnp.int32)
    ranking = jnp.cumsum(belongs) - 1
    matched = (belongs[None, :] == 1) & (
        ranking[None, :] == jnp.arange(CAP, dtype=jnp.int32)[:, None]
    )
    slot_owner = jnp.sum(
        matched.astype(jnp.int32) * jnp.arange(seq_total, dtype=jnp.int32)[None, :], axis=1
    )
    occupied = jnp.any(matched, axis=1)
    local_count = cached_blocks.shape[0]
    owned = worker_index * local_count + jnp.arange(local_count, dtype=jnp.int32)
    mixed = attend(
        tokens,
        cached_blocks,
        jnp.take(cache_length, owned),
        jnp.take(block_table, owned, axis=0),
        norm_gain,
        query_weight,
        key_weight,
        value_weight,
        output_weight,
    )
    everyone = lax.all_gather(mixed, "worker", axis=0, tiled=True)
    placed = jnp.take(everyone.reshape(seq_total, NEW, -1), slot_owner, axis=0)
    result = jnp.where(occupied[:, None, None], placed, jnp.zeros_like(placed))
    return result[None]


def solution(mesh):
    placed = (
        P(("groups", "worker"), "tensor"),
        P(),
        P(None, "tensor"),
        P(None, "tensor"),
        P(None, "tensor"),
        P("tensor", None),
        P(("groups", "worker"), "tensor", None, None),
        P("groups"),
        P("groups", None),
        P("groups"),
    )
    return jax.shard_map(
        local,
        mesh=mesh,
        in_specs=placed,
        out_specs=P(("groups", "worker"), None, None, "tensor"),
        check_vma=False,
    )
```

profile of v0, /device:TPU:0, one launch (start us, length us, event | category | flops | bytes accessed | tf_op | source)
XLA Modules:
  0.0 310.5 jit_solution(4129475814052174620)
XLA Ops:
  6.5 0.0 copy-start
  6.5 0.0 all-gather.3.cloned.1.call-start
  6.5 0.7 all-gather.3.cloned.1.call-update
  7.3 2.6 copy.86
  9.8 1.3 copy.87
  11.1 7.3 %all-to-all-start = ((bf16[2,128,2,8,128]{4,1,0,2,3:T(8,128)(2,1)}), bf16[2,128,2,8,128]{4,1,0,2,3:T(8,128)(2,1)S(1)}, u32[]{:S(2)}, u32[]{:S(2)}) async-start(bf16[2,128,2,8,128]{4,1,0,2,3:T(8,128)(2,1)} %copy.87), calls=%async_computation | async-start | bytes 2097152 | tf_op jit(solution)/shard_map/all_to_all | solution.py:97
  18.4 0.0 reduce-scatter.2.cloned.1.call-start
  18.5 1.3 gather_fusion.2
  19.8 1.3 gather_fusion
  21.1 0.1 broadcast_select_fusion
  21.2 0.1 copy.80
  21.3 4.0 %gather_fusion.1 = s32[1024,2]{1,0:T(8,128)} fusion(s32[2,64]{0,1:T(8,128)S(1)} %copy.80, s32[1024]{0:T(1024)S(1)} %broadcast_clamp_fusion), kind=kCustom, calls=%fused_computation.1 | custom fusion | bytes 20480 | tf_op jit(solution)/shard_map/jit(_take)/gather | solution.py:102
  25.3 1.2 copy.81
  26.6 0.6 iota_compare_fusion
  27.2 0.1 fusion.68
  27.3 0.5 multiply_cosine_fusion
  27.8 0.1 pad_maximum_fusion
  28.0 0.1 compare_bitcast_fusion
  28.0 0.3 multiply_sine_fusion.1
  28.3 32.7 %all-to-all-done = bf16[2,128,2,8,128]{4,1,0,2,3:T(8,128)(2,1)S(1)} async-done(((bf16[2,128,2,8,128]{4,1,0,2,3:T(8,128)(2,1)}), bf16[2,128,2,8,128]{4,1,0,2,3:T(8,128)(2,1)S(1)}, u32[]{:S(2)}, u32[]{:S(2)}) %all-to-all-start) | async-done | bytes 1048608 | tf_op jit(solution)/shard_map/all_to_all | solution.py:97
  61.1 1.0 copy.88
  62.1 40.3 %all-gather.3.cloned.1.call-done = bf16[256,8192]{1,0:T(8,128)(2,1)} async-done(((bf16[256,1024]{1,0:T(8,128)(2,1)}), bf16[256,8192]{1,0:T(8,128)(2,1)}) %all-gather.3.cloned.1.call-update) | async-done | bytes 4194320 | tf_op jit(solution)/shard_map/all_gather | solution.py:54
  102.4 3.1 fusion.1
  105.5 0.0 copy-done
  105.5 3.6 %fusion.25 = bf16[256,128]{0,1:T(8,128)(2,1)S(1)} fusion(bf16[8192,128]{1,0:T(8,128)(2,1)S(1)} %copy-done, bf16[256,8192]{1,0:T(8,128)(2,1)} %all-gather.3.cloned.1.call-done, f32[8192]{0:T(1024)} %param.11, f32[256]{0:T(256)S(1)} %add_rsqrt_fusion), kind=kOutput, calls=%fused_computation.28 | convolution fusion | flops 543227904 | bytes 6390784 | tf_op jit(solution)/shard_map/dot_general | solution.py:58
  109.1 0.6 reshape.302
  109.7 0.0 copy-done.6
  109.7 4.3 %fusion.31 = f32[256,128]{0,1:T(8,128)S(1)} fusion(bf16[8192,128]{1,0:T(8,128)(2,1)} %param.13, bf16[256,8192]{1,0:T(8,128)(2,1)} %all-gather.3.cloned.1.call-done, f32[8192]{0:T(1024)S(1)} %copy-done.6, f32[256]{0:T(256)S(1)} %add_rsqrt_fusion), kind=kOutput, calls=%fused_computation.30 | convolution fusion | flops 543260672 | bytes 6456320 | tf_op jit(solution)/shard_map/dot_general | solution.py:57
  114.1 0.1 copy.106
  114.2 9.5 %fusion.11 = f32[256,1024]{1,0:T(8,128)S(1)} fusion(bf16[8192,1024]{1,0:T(8,128)(2,1)} %param.12, bf16[256,8192]{1,0:T(8,128)(2,1)} %all-gather.3.cloned.1.call-done, f32[8192]{0:T(1024)} %param.11, f32[256]{0:T(256)S(1)} %add_rsqrt_fusion), kind=kOutput, calls=%fused_computation.18 | convolution fusion | flops 4301520896 | bytes 22053888 | tf_op jit(solution)/shard_map/dot_general | solution.py:56
  123.8 0.3 copy.109
  124.1 0.2 copy.110
  124.3 0.9 slice_negate_fusion
  125.2 0.4 copy.104
  125.6 1.5 copy.105
  127.1 0.4 fusion.35
  127.5 0.3 fusion.69
  127.8 0.0 copy-start.2
  127.8 2.6 bitcast_reduce_fusion
  130.5 0.2 fusion.36
  130.6 0.0 slice-start
  130.6 2.1 fusion.3
  132.8 0.0 slice-start.1
  132.8 0.0 slice-start.2
  132.8 0.0 slice-start.3
  132.8 2.5 fusion.17
  135.3 0.4 fusion.18
  135.7 0.3 copy.96
  136.1 0.1 slice-done.2
  136.2 1.2 slice-done.3
  137.4 6.7 %fusion.38 = f32[256,8192]{1,0:T(8,128)} fusion(bf16[1024,8192]{1,0:T(8,128)(2,1)S(1)} %bitcast.101, bf16[32,8,8,128]{3,2,1,0:T(8,128)(2,1)S(1)} %bitcast.109), kind=kOutput, calls=%fused_computation.40 | convolution fusion | flops 4294967296 | bytes 25690112 | tf_op jit(solution)/shard_map/dot_general | solution.py:125
  144.1 0.0 reduce-scatter.2.cloned.1.call-update
  144.2 0.0 all-gather.5.cloned.1.call-start
  144.2 146.5 %reduce-scatter.2.cloned.1.call-done = f32[256,1024]{1,0:T(8,128)} async-done(((f32[256,8192]{1,0:T(8,128)}), f32[256,1024]{1,0:T(8,128)}) %reduce-scatter.2.cloned.1.call-update) | async-done | bytes 1048592 | tf_op jit(solution)/shard_map/reduce_scatter | solution.py:126
  290.7 2.1 convert_element_type.67
  292.8 0.0 all-gather.5.cloned.1.call-update
  292.8 0.0 copy-done.5
  292.8 0.2 reduce-window.8
  293.0 0.1 select_reduce_fusion
  293.2 0.1 fusion.61
  293.3 7.8 %all-gather.5.cloned.1.call-done = bf16[512,1024]{1,0:T(8,128)(2,1)} async-done(((bf16[256,1024]{1,0:T(8,128)(2,1)}), bf16[512,1024]{1,0:T(8,128)(2,1)}) %all-gather.5.cloned.1.call-update) | async-done | bytes 1048592 | tf_op jit(solution)/shard_map/all_gather | solution.py:166
  301.1 1.8 gather_fusion.3
  302.9 1.0 fusion.37
  304.0 0.0 copy-done.1
  (30 shorter events, 0.2 us)
Async XLA Ops:
  6.5 98.9 %copy-start = (bf16[8192,128]{1,0:T(8,128)(2,1)S(1)}, bf16[8192,128]{1,0:T(8,128)(2,1)}, u32[]{:S(2)}) copy-start(bf16[8192,128]{1,0:T(8,128)(2,1)} %param.14) | copy-start | bytes 6291460
  6.5 95.8 %all-gather.3.cloned.1.call-start = ((), (), s32[]{:S(2)}) async-start(), calls=%async_computation.2 | async-start | bytes 4718592 | tf_op jit(solution)/shard_map/all_gather | solution.py:54
  11.1 49.9 %all-to-all-start = ((bf16[2,128,2,8,128]{4,1,0,2,3:T(8,128)(2,1)}), bf16[2,128,2,8,128]{4,1,0,2,3:T(8,128)(2,1)S(1)}, u32[]{:S(2)}, u32[]{:S(2)}) async-start(bf16[2,128,2,8,128]{4,1,0,2,3:T(8,128)(2,1)} %copy.87), calls=%async_computation | async-start | bytes 2097152 | tf_op jit(solution)/shard_map/all_to_all | solution.py:97
  18.4 272.2 %reduce-scatter.2.cloned.1.call-start = ((), (), s32[]{:S(2)}) async-start(), calls=%async_computation.3 | async-start | bytes 9437184 | tf_op jit(solution)/shard_map/reduce_scatter | solution.py:126
  62.1 47.6 %copy-start.6 = (f32[8192]{0:T(1024)S(1)}, f32[8192]{0:T(1024)}, u32[]{:S(2)}) copy-start(f32[8192]{0:T(1024)} %param.11) | copy-start | bytes 98308
  123.8 3.7 %copy-start.3 = (pred[128,128]{0,1:T(8,128)(4,1)S(1)}, pred[128,128]{0,1:T(8,128)(4,1)}, u32[]{:S(2)}) copy-start(pred[128,128]{0,1:T(8,128)(4,1)} %iota_compare_fusion) | copy-start | bytes 49156
  127.8 4.9 %copy-start.2 = (bf16[2,8,128,2,1,128]{5,2,1,0,3,4:T(8,128)(2,1)S(1)}, bf16[2,8,128,2,1,128]{5,2,1,0,3,4:T(8,128)(2,1)}, u32[]{:S(2)}) copy-start(bf16[2,8,128,2,1,128]{5,2,1,0,3,4:T(8,128)(2,1)} %copy.88) | copy-start | bytes 3145732
  130.6 5.4 %slice-start = ((s8[16777216]{0:T(1024)(128)(4,1)}), s8[4194304]{0:T(1024)(128)(4,1)S(1)}, s32[]{:S(2)}) async-start(s8[16777216]{0:T(1024)(128)(4,1)} %bitcast.100), calls=%async_computation.5 | async-start | bytes 8388608
  132.8 2.5 copy-start.4
  132.8 3.3 %slice-start.1 = ((s8[16777216]{0:T(1024)(128)(4,1)}), s8[4194304]{0:T(1024)(128)(4,1)S(1)}, s32[]{:S(2)}) async-start(s8[16777216]{0:T(1024)(128)(4,1)} %bitcast.100), calls=%async_computation.6 | async-start | bytes 8388608
  132.8 3.4 %slice-start.2 = ((s8[16777216]{0:T(1024)(128)(4,1)}), s8[4194304]{0:T(1024)(128)(4,1)S(1)}, s32[]{:S(2)}) async-start(s8[16777216]{0:T(1024)(128)(4,1)} %bitcast.100), calls=%async_computation.7 | async-start | bytes 8388608
  132.8 4.6 %slice-start.3 = ((s8[16777216]{0:T(1024)(128)(4,1)}), s8[4194304]{0:T(1024)(128)(4,1)S(1)}, s32[]{:S(2)}) async-start(s8[16777216]{0:T(1024)(128)(4,1)} %bitcast.100), calls=%async_computation.8 | async-start | bytes 8388608
  137.4 166.6 %copy-start.1 = (bf16[8192,128]{1,0:T(8,128)(2,1)S(1)}, bf16[8192,128]{1,0:T(8,128)(2,1)}, u32[]{:S(2)}) copy-start(bf16[8192,128]{1,0:T(8,128)(2,1)} %param.14) | copy-start | bytes 6291460
  144.1 148.7 %copy-start.5 = (s32[4]{0:T(128)S(1)}, s32[4]{0:T(128)}, u32[]{:S(2)}) copy-start(s32[4]{0:T(128)} %param.19) | copy-start | bytes 52
  144.2 156.9 %all-gather.5.cloned.1.call-start = ((), (), s32[]{:S(2)}) async-start(), calls=%async_computation.4 | async-start | bytes 1572864 | tf_op jit(solution)/shard_map/all_gather | solution.py:166
Sparse Core Ops, SparseCore 0:
  9.5 92.8 all-gather.2
  144.3 146.3 reduce-scatter.1
  292.9 8.1 all-gather.4
where the time goes:
time: 311 us; the launch traced here: 310 us
  waiting for transfers between devices  228 us (73%)
  matrix products  30 us (10%)
  local copies, waits for them, and re-layouts  19.5 us (6%)
  between operations  13.5 us (4%)
  other arithmetic  12.2 us (4%)
  starting transfers between devices  7.39 us (2%)
    reduce_scatter x1, waiting for transfers between devices, attend(): lax.psum_scatter(partial_value, 'tensor', scatter_dimension=1, tiled=True)  146 us
    all_gather x1, waiting for transfers between devices, attend(): lax.all_gather(token_rows, 'tensor', axis=1, tiled=True).astype(jnp.float32)  40.3 us
    all_to_all x1, waiting for transfers between devices, attend(): lax.all_to_all(spread, 'tensor', split_axis=3, concat_axis=1, tiled=True)  32.7 us
    dot_general x1, matrix products, attend(): jnp.dot(scaled, query_weight, preferred_element_type=jnp.float32)  9.52 us
    all_gather x1, waiting for transfers between devices, local(): everyone = lax.all_gather(mixed, 'worker', axis=0, tiled=True)  7.81 us
    all_to_all x1, starting transfers between devices, attend(): lax.all_to_all(spread, 'tensor', split_axis=3, concat_axis=1, tiled=True)  7.31 us
    dot_general x1, matrix products, attend(): jnp.dot(attended_rows, output_weight, preferred_element_type=jnp.float32)  6.74 us
  transfers between devices with their start and end apart: 4, of which 4 were waited for; matrix products, arithmetic and copies ran while one was open for 5% of the time, Pallas kernels for 0%

commit v1 on v0

--- a/solution.py
+++ b/solution.py
@@ -11,6 +11,16 @@
 BLK = 16
 CAP = 3
 epsilon = 1e-05
+
+
+def collect(x, axis, dim):
+    ways, here, step = (lax.axis_size(axis), lax.axis_index(axis), x.shape[dim])
+    lengths = [n * ways if d == dim else n for d, n in enumerate(x.shape)]
+    full = lax.dynamic_update_slice_in_dim(jnp.zeros(lengths, x.dtype), x, here * step, axis=dim)
+    for far in range(1, ways):
+        x = lax.ppermute(x, axis, [(d, (d + 1) % ways) for d in range(ways)])
+        full = lax.dynamic_update_slice_in_dim(full, x, (here - far) % ways * step, axis=dim)
+    return full
 
 
 def from_partner(block, axis, bit):
@@ -51,7 +61,7 @@
     seq_count = blocks.shape[0]
     total = token_rows.shape[0]
     query_cols = query_weight.shape[1]
-    widened = lax.all_gather(token_rows, "tensor", axis=1, tiled=True).astype(jnp.float32)
+    widened = collect(token_rows, "tensor", 1).astype(jnp.float32)
     scaled = (widened * norm_gain[None, :]).astype(jnp.bfloat16)
     query_sum = jnp.dot(scaled, query_weight, preferred_element_type=jnp.float32)
     key_sum = jnp.dot(scaled, key_weight, preferred_element_type=jnp.float32)

time: 311 us -> 335 us (1.077)
  local copies, waits for them, and re-layouts: 19.5 us -> 35.6 us
  starting transfers between devices: 7.39 us -> 11.6 us
  waiting for transfers between devices: 228 us -> 232 us
    ppermute x0 -> x7, waiting for transfers between devices: none -> 77.9 us  [collect(): x = lax.ppermute(x, axis, [(d, (d + 1) % ways) for d in range(ways)])]
    all_gather x1 -> x0, waiting for transfers between devices: 40.3 us -> none  [attend(): lax.all_gather(token_rows, 'tensor', axis=1, tiled=True).astype(jnp.float32)]
    all_to_all x1, waiting for transfers between devices: 32.7 us -> 0.01 us  [attend(): lax.all_to_all(spread, 'tensor', split_axis=3, concat_axis=1, tiled=True)]
    dynamic_update_slice x0 -> x8, local copies, waits for them, and re-layouts: none -> 14.3 us  [the longest x7 13.4 us: collect(): lax.dynamic_update_slice_in_dim(full, x, (here - far) % ways * step, axis...]
    ppermute x0 -> x7, starting transfers between devices: none -> 6.69 us  [collect(): x = lax.ppermute(x, axis, [(d, (d + 1) % ways) for d in range(ways)])]
  transfers between devices with their start and end apart: 4 -> 10, of which waited for: 4 -> 9; matrix products, arithmetic and copies ran while one was open for 5% -> 9% of each run, Pallas kernels for 0% -> 0%
where the time goes in v1:
time: 335 us
  waiting for transfers between devices  232 us (69%)
  local copies, waits for them, and re-layouts  35.6 us (11%)
  matrix products  28.9 us (9%)
  between operations  13.8 us (4%)
  other arithmetic  12.2 us (4%)
  starting transfers between devices  11.6 us (3%)
    reduce_scatter x1, waiting for transfers between devices, attend(): lax.psum_scatter(partial_value, 'tensor', scatter_dimension=1, tiled=True)  147 us
    ppermute x7, waiting for transfers between devices, collect(): x = lax.ppermute(x, axis, [(d, (d + 1) % ways) for d in range(ways)])  77.9 us
    dynamic_update_slice x7, local copies, waits for them, and re-layouts, collect(): lax.dynamic_update_slice_in_dim(full, x, (here - far) % ways * step, axis...  13.4 us
    dot_general x1, matrix products, attend(): jnp.dot(scaled, query_weight, preferred_element_type=jnp.float32)  9.67 us
    all_gather x1, waiting for transfers between devices, local(): everyone = lax.all_gather(mixed, 'worker', axis=0, tiled=True)  7.81 us
    dot_general x1, matrix products, attend(): jnp.dot(attended_rows, output_weight, preferred_element_type=jnp.float32)  6.79 us
  transfers between devices with their start and end apart: 10, of which 9 were waited for; matrix products, arithmetic and copies ran while one was open for 9% of the time, Pallas kernels for 0%

profile of v1, /device:TPU:0, one launch (start us, length us, event | category | flops | bytes accessed | tf_op | source)
XLA Modules:
  0.0 334.5 jit_solution(6947151480349560737)
XLA Ops:
  6.5 3.0 collective-permute-start
  9.5 2.5 copy.86
  12.1 1.3 copy.87
  13.4 4.9 %all-to-all-start = ((bf16[2,128,2,8,128]{4,1,0,2,3:T(8,128)(2,1)}), bf16[2,128,2,8,128]{4,1,0,2,3:T(8,128)(2,1)S(1)}, u32[]{:S(2)}, u32[]{:S(2)}) async-start(bf16[2,128,2,8,128]{4,1,0,2,3:T(8,128)(2,1)} %copy.87), calls=%async_computation | async-start | bytes 2097152 | tf_op jit(solution)/shard_map/all_to_all | solution.py:107
  18.3 8.2 %collective-permute-done = bf16[256,1024]{1,0:T(8,128)(2,1)} collective-permute-done((bf16[256,1024]{1,0:T(8,128)(2,1)}, bf16[256,1024]{1,0:T(8,128)(2,1)}, u32[]{:S(2)}, u32[]{:S(2)}) %collective-permute-start) | collective-permute-done | bytes 524320 | tf_op jit(solution)/shard_map/ppermute | solution.py:21
  26.5 3.7 %collective-permute-start.1 = (bf16[256,1024]{1,0:T(8,128)(2,1)}, bf16[256,1024]{1,0:T(8,128)(2,1)}, u32[]{:S(2)}, u32[]{:S(2)}) collective-permute-start(bf16[256,1024]{1,0:T(8,128)(2,1)} %collective-permute-done), channel_id=1, source_target_pairs={{0,1},{1,2},{2,3},{3,4},{4,5},{5,6},{6,7},{7,0},{8,9},{9,10},{10,1... | collective-permute-start | bytes 1572872 | tf_op jit(solution)/shard_map/ppermute | solution.py:21
  30.2 0.6 gather_fusion.2
  30.9 0.6 gather_fusion
  31.5 0.1 copy.80
  31.6 21.5 %collective-permute-done.1 = bf16[256,1024]{1,0:T(8,128)(2,1)} collective-permute-done((bf16[256,1024]{1,0:T(8,128)(2,1)}, bf16[256,1024]{1,0:T(8,128)(2,1)}, u32[]{:S(2)}, u32[]{:S(2)}) %collective-permute-start.1) | collective-permute-done | bytes 524320 | tf_op jit(solution)/shard_map/ppermute | solution.py:21
  53.2 4.0 %gather_fusion.1 = s32[1024,2]{1,0:T(8,128)} fusion(s32[2,64]{0,1:T(8,128)S(1)} %copy.80, s32[1024]{0:T(1024)S(1)} %broadcast_clamp_fusion), kind=kCustom, calls=%fused_computation.1 | custom fusion | bytes 20480 | tf_op jit(solution)/shard_map/jit(_take)/gather | solution.py:112
  57.2 1.2 copy.81
  58.4 10.8 %collective-permute-done.2 = bf16[256,1024]{1,0:T(8,128)(2,1)} collective-permute-done((bf16[256,1024]{1,0:T(8,128)(2,1)}, bf16[256,1024]{1,0:T(8,128)(2,1)}, u32[]{:S(2)}, u32[]{:S(2)}) %collective-permute-start.2) | collective-permute-done | bytes 524320 | tf_op jit(solution)/shard_map/ppermute | solution.py:21
  69.4 15.0 %collective-permute-done.3 = bf16[256,1024]{1,0:T(8,128)(2,1)S(1)} collective-permute-done((bf16[256,1024]{1,0:T(8,128)(2,1)}, bf16[256,1024]{1,0:T(8,128)(2,1)S(1)}, u32[]{:S(2)}, u32[]{:S(2)}) %collective-permute-start.3) | collective-permute-done | bytes 524320 | tf_op jit(solution)/shard_map/ppermute | solution.py:21
  84.4 0.5 multiply_cosine_fusion
  84.9 0.3 copy-done.5
  85.1 0.1 pad_maximum_fusion
  85.3 0.1 compare_bitcast_fusion
  85.4 13.1 %collective-permute-done.4 = bf16[256,1024]{1,0:T(8,128)(2,1)} collective-permute-done((bf16[256,1024]{1,0:T(8,128)(2,1)S(1)}, bf16[256,1024]{1,0:T(8,128)(2,1)}, u32[]{:S(2)}, u32[]{:S(2)}) %collective-permute-start.4) | collective-permute-done | bytes 524320 | tf_op jit(solution)/shard_map/ppermute | solution.py:21
  98.5 0.6 iota_compare_fusion
  99.1 2.4 broadcast_in_dim.106
  101.5 0.9 constant_dynamic-update-slice_fusion.7
  102.4 0.3 multiply_sine_fusion.1
  102.7 1.9 constant_dynamic-update-slice_fusion.6
  104.6 7.3 %collective-permute-done.5 = bf16[256,1024]{1,0:T(8,128)(2,1)} collective-permute-done((bf16[256,1024]{1,0:T(8,128)(2,1)}, bf16[256,1024]{1,0:T(8,128)(2,1)}, u32[]{:S(2)}, u32[]{:S(2)}) %collective-permute-start.5) | collective-permute-done | bytes 524320 | tf_op jit(solution)/shard_map/ppermute | solution.py:21
  111.9 1.9 constant_dynamic-update-slice_fusion.5
  113.8 1.9 constant_dynamic-update-slice_fusion.4
  115.7 1.1 copy.88
  116.8 1.9 constant_dynamic-update-slice_fusion.3
  118.8 1.9 constant_dynamic-update-slice_fusion.2
  120.7 1.9 constant_dynamic-update-slice_fusion.1
  122.6 2.0 collective-permute-done.6
  124.5 1.9 constant_dynamic-update-slice_fusion
  126.5 3.1 fusion.1
  129.6 3.6 %fusion.25 = bf16[256,128]{0,1:T(8,128)(2,1)S(1)} fusion(bf16[8192,128]{1,0:T(8,128)(2,1)S(1)} %copy-done, bf16[256,8192]{1,0:T(8,128)(2,1)} %constant_dynamic-update-slice_fusion, f32[8192]{0:T(1024)S(1)} %copy-done.10, f32[256]{0:T(256)S(1)} %add_rsqrt_fusion), kind=kOutput, calls=%fused_computation.28 | convolution fusion | flops 543227904 | bytes 6390784 | tf_op jit(solution)/shard_map/dot_general | solution.py:68
  133.2 0.6 reshape.302
  133.9 4.3 %fusion.31 = f32[256,128]{0,1:T(8,128)S(1)} fusion(bf16[8192,128]{1,0:T(8,128)(2,1)} %param.13, bf16[256,8192]{1,0:T(8,128)(2,1)} %constant_dynamic-update-slice_fusion, f32[8192]{0:T(1024)S(1)} %copy-done.10, f32[256]{0:T(256)S(1)} %add_rsqrt_fusion), kind=kOutput, calls=%fused_computation.30 | convolution fusion | flops 543260672 | bytes 6456320 | tf_op jit(solution)/shard_map/dot_general | solution.py:67
  138.2 0.1 copy.106
  138.4 9.7 %fusion.11 = f32[256,1024]{1,0:T(8,128)S(1)} fusion(bf16[8192,1024]{1,0:T(8,128)(2,1)} %param.12, bf16[256,8192]{1,0:T(8,128)(2,1)} %constant_dynamic-update-slice_fusion, f32[8192]{0:T(1024)S(1)} %copy-done.10, f32[256]{0:T(256)S(1)} %add_rsqrt_fusion), kind=kOutput, calls=%fused_computation.18 | convolution fusion | flops 4301520896 | bytes 22053888 | tf_op jit(solution)/shard_map/dot_general | solution.py:66
  148.0 0.3 copy.109
  148.4 0.9 slice_negate_fusion
  149.3 0.4 copy.104
  149.7 1.5 copy.105
  151.2 0.2 copy.110
  151.4 0.5 fusion.35
  151.9 0.3 fusion.69
  152.2 0.2 copy-done.3
  152.4 1.5 bitcast_reduce_fusion
  153.9 0.2 fusion.36
  154.1 2.1 fusion.3
  156.3 2.3 fusion.17
  158.6 0.4 fusion.18
  159.0 0.3 copy.96
  159.3 0.3 slice-done.2
  159.6 1.2 slice-done.3
  160.8 6.8 %fusion.38 = f32[256,8192]{1,0:T(8,128)} fusion(bf16[1024,8192]{1,0:T(8,128)(2,1)S(1)} %bitcast.101, bf16[32,8,8,128]{3,2,1,0:T(8,128)(2,1)S(1)} %bitcast.109), kind=kOutput, calls=%fused_computation.40 | convolution fusion | flops 4294967296 | bytes 25690112 | tf_op jit(solution)/shard_map/dot_general | solution.py:135
  167.7 146.7 %reduce-scatter.2.cloned.1.call-done = f32[256,1024]{1,0:T(8,128)} async-done(((f32[256,8192]{1,0:T(8,128)}), f32[256,1024]{1,0:T(8,128)}) %reduce-scatter.2.cloned.1.call-update) | async-done | bytes 1048592 | tf_op jit(solution)/shard_map/reduce_scatter | solution.py:136
  314.4 2.1 convert_element_type.67
  316.6 0.2 reduce-window.8
  316.8 0.1 select_reduce_fusion
  316.9 0.1 fusion.61
  317.0 7.8 %all-gather.2.cloned.1.call-done = bf16[512,1024]{1,0:T(8,128)(2,1)} async-done(((bf16[256,1024]{1,0:T(8,128)(2,1)}), bf16[512,1024]{1,0:T(8,128)(2,1)}) %all-gather.2.cloned.1.call-update) | async-done | bytes 1048592 | tf_op jit(solution)/shard_map/all_gather | solution.py:176
  324.8 1.8 gather_fusion.3
  326.7 1.0 fusion.37
  (58 shorter events, 0.5 us)
Async XLA Ops:
  6.5 123.0 %copy-start = (bf16[8192,128]{1,0:T(8,128)(2,1)S(1)}, bf16[8192,128]{1,0:T(8,128)(2,1)}, u32[]{:S(2)}) copy-start(bf16[8192,128]{1,0:T(8,128)(2,1)} %param.14) | copy-start | bytes 6291460
  6.5 23.7 %copy-start.2 = (s32[4]{0:T(128)S(1)}, s32[4]{0:T(128)}, u32[]{:S(2)}) copy-start(s32[4]{0:T(128)} %param.17) | copy-start | bytes 52
  6.5 24.3 %copy-start.8 = (s32[4,64]{1,0:T(4,128)S(1)}, s32[4,64]{1,0:T(4,128)}, u32[]{:S(2)}) copy-start(s32[4,64]{1,0:T(4,128)} %param.18) | copy-start | bytes 3076
  6.5 20.0 %collective-permute-start = (bf16[256,1024]{1,0:T(8,128)(2,1)}, bf16[256,1024]{1,0:T(8,128)(2,1)}, u32[]{:S(2)}, u32[]{:S(2)}) collective-permute-start(bf16[256,1024]{1,0:T(8,128)(2,1)} %param.10), channel_id=1, source_target_pairs={{0,1},{1,2},{2,3},{3,4},{4,5},{5,6},{6,7},{7,0},{8,9},{9,10},{10,1... | collective-permute-start | bytes 1572872 | tf_op jit(solution)/shard_map/ppermute | solution.py:21
  13.4 102.3 %all-to-all-start = ((bf16[2,128,2,8,128]{4,1,0,2,3:T(8,128)(2,1)}), bf16[2,128,2,8,128]{4,1,0,2,3:T(8,128)(2,1)S(1)}, u32[]{:S(2)}, u32[]{:S(2)}) async-start(bf16[2,128,2,8,128]{4,1,0,2,3:T(8,128)(2,1)} %copy.87), calls=%async_computation | async-start | bytes 2097152 | tf_op jit(solution)/shard_map/all_to_all | solution.py:107
  18.3 296.1 %reduce-scatter.2.cloned.1.call-start = ((), (), s32[]{:S(2)}) async-start(), calls=%async_computation.2 | async-start | bytes 9437184 | tf_op jit(solution)/shard_map/reduce_scatter | solution.py:136
  26.5 26.6 %collective-permute-start.1 = (bf16[256,1024]{1,0:T(8,128)(2,1)}, bf16[256,1024]{1,0:T(8,128)(2,1)}, u32[]{:S(2)}, u32[]{:S(2)}) collective-permute-start(bf16[256,1024]{1,0:T(8,128)(2,1)} %collective-permute-done), channel_id=1, source_target_pairs={{0,1},{1,2},{2,3},{3,4},{4,5},{5,6},{6,7},{7,0},{8,9},{9,10},{10,1... | collective-permute-start | bytes 1572872 | tf_op jit(solution)/shard_map/ppermute | solution.py:21
  53.1 16.1 %collective-permute-start.2 = (bf16[256,1024]{1,0:T(8,128)(2,1)}, bf16[256,1024]{1,0:T(8,128)(2,1)}, u32[]{:S(2)}, u32[]{:S(2)}) collective-permute-start(bf16[256,1024]{1,0:T(8,128)(2,1)} %collective-permute-done.1), channel_id=1, source_target_pairs={{0,1},{1,2},{2,3},{3,4},{4,5},{5,6},{6,7},{7,0},{8,9},{9,10},{10,1... | collective-permute-start | bytes 1572872 | tf_op jit(solution)/shard_map/ppermute | solution.py:21
  69.3 15.1 %collective-permute-start.3 = (bf16[256,1024]{1,0:T(8,128)(2,1)}, bf16[256,1024]{1,0:T(8,128)(2,1)S(1)}, u32[]{:S(2)}, u32[]{:S(2)}) collective-permute-start(bf16[256,1024]{1,0:T(8,128)(2,1)} %collective-permute-done.2), channel_id=1, source_target_pairs={{0,1},{1,2},{2,3},{3,4},{4,5},{5,6},{6,7},{7,0},{8,9},{9,10},{10,1... | collective-permute-start | bytes 1572872 | tf_op jit(solution)/shard_map/ppermute | solution.py:21
  84.3 0.8 copy-start.5
  84.4 14.1 %collective-permute-start.4 = (bf16[256,1024]{1,0:T(8,128)(2,1)S(1)}, bf16[256,1024]{1,0:T(8,128)(2,1)}, u32[]{:S(2)}, u32[]{:S(2)}) collective-permute-start(bf16[256,1024]{1,0:T(8,128)(2,1)S(1)} %collective-permute-done.3), channel_id=1, source_target_pairs={{0,1},{1,2},{2,3},{3,4},{4,5},{5,6},{6,7},{7,0},{8,9},{9,10},{10,1... | collective-permute-start | bytes 1572872 | tf_op jit(solution)/shard_map/ppermute | solution.py:21
  98.5 13.5 %collective-permute-start.5 = (bf16[256,1024]{1,0:T(8,128)(2,1)}, bf16[256,1024]{1,0:T(8,128)(2,1)}, u32[]{:S(2)}, u32[]{:S(2)}) collective-permute-start(bf16[256,1024]{1,0:T(8,128)(2,1)} %collective-permute-done.4), channel_id=1, source_target_pairs={{0,1},{1,2},{2,3},{3,4},{4,5},{5,6},{6,7},{7,0},{8,9},{9,10},{10,1... | collective-permute-start | bytes 1572872 | tf_op jit(solution)/shard_map/ppermute | solution.py:21
  99.1 2.4 copy-start.4
  111.9 12.6 %collective-permute-start.6 = (bf16[256,1024]{1,0:T(8,128)(2,1)}, bf16[256,1024]{1,0:T(8,128)(2,1)}, u32[]{:S(2)}, u32[]{:S(2)}) collective-permute-start(bf16[256,1024]{1,0:T(8,128)(2,1)} %collective-permute-done.5), channel_id=1, source_target_pairs={{0,1},{1,2},{2,3},{3,4},{4,5},{5,6},{6,7},{7,0},{8,9},{9,10},{10,1... | collective-permute-start | bytes 1572872 | tf_op jit(solution)/shard_map/ppermute | solution.py:21
  116.8 12.7 %copy-start.10 = (f32[8192]{0:T(1024)S(1)}, f32[8192]{0:T(1024)}, u32[]{:S(2)}) copy-start(f32[8192]{0:T(1024)} %param.11) | copy-start | bytes 98308
  149.7 2.2 copy-start.6
  151.2 1.2 copy-start.3
  154.1 5.2 %slice-start = ((s8[16777216]{0:T(1024)(128)(4,1)}), s8[4194304]{0:T(1024)(128)(4,1)S(1)}, s32[]{:S(2)}) async-start(s8[16777216]{0:T(1024)(128)(4,1)} %bitcast.100), calls=%async_computation.4 | async-start | bytes 8388608
  156.2 2.3 copy-start.7
  156.2 3.1 slice-start.1
  156.2 3.4 %slice-start.2 = ((s8[16777216]{0:T(1024)(128)(4,1)}), s8[4194304]{0:T(1024)(128)(4,1)S(1)}, s32[]{:S(2)}) async-start(s8[16777216]{0:T(1024)(128)(4,1)} %bitcast.100), calls=%async_computation.6 | async-start | bytes 8388608
  156.3 4.6 %slice-start.3 = ((s8[16777216]{0:T(1024)(128)(4,1)}), s8[4194304]{0:T(1024)(128)(4,1)S(1)}, s32[]{:S(2)}) async-start(s8[16777216]{0:T(1024)(128)(4,1)} %bitcast.100), calls=%async_computation.7 | async-start | bytes 8388608
  167.6 148.9 %copy-start.9 = (s32[4]{0:T(128)S(1)}, s32[4]{0:T(128)}, u32[]{:S(2)}) copy-start(s32[4]{0:T(128)} %param.19) | copy-start | bytes 52
  167.6 160.1 %copy-start.1 = (bf16[8192,128]{1,0:T(8,128)(2,1)S(1)}, bf16[8192,128]{1,0:T(8,128)(2,1)}, u32[]{:S(2)}) copy-start(bf16[8192,128]{1,0:T(8,128)(2,1)} %param.14) | copy-start | bytes 6291460
  167.7 157.2 %all-gather.2.cloned.1.call-start = ((), (), s32[]{:S(2)}) async-start(), calls=%async_computation.3 | async-start | bytes 1572864 | tf_op jit(solution)/shard_map/all_gather | solution.py:176
Sparse Core Ops, SparseCore 0:
  167.8 146.6 reduce-scatter.1
  316.7 8.1 all-gather.1
